TPU v7x, 128 devices: a whole 4x4x4 slice. The times are simulated.
128 devices in a mesh: ctx: 16 (over y, z_hi, core), tp: 8 (over z_lo, x).
Axes of the slice: x: 4, y: 4, z: 4 (z_hi: 2, z_lo: 2; z = z_hi * 2 + z_lo), core: 2. Of those that a mesh axis runs over, the one named last changes fastest.
Arguments:
- prompt_states: bfloat16 [2048, 1024], P('ctx'), may hold values from -1.5 to 1.5
- segment_ids: int32 [2048], P('ctx'), may hold values from 0 to 3, never falling along the last dimension, each value on 1 to 1024 neighbouring positions
- past_keys: bfloat16 [2048, 1024], P('ctx', 'tp'), may hold values from -1024 to 1024
- past_values: bfloat16 [2048, 1024], P('ctx', 'tp'), may hold values from -6 to 6
- cache_request: int32 [2048], P('ctx'), may hold values from 0 to 2, as said below
- decode_ids: int32 [4], replicated, may hold values from 0 to 32127
- embed_table: bfloat16 [32128, 1024], P(('ctx', 'tp')), may hold values from -6 to 6
- attn_gain: bfloat16 [1024], replicated, may hold values from 0.25 to 1.75
- ff_gain: bfloat16 [1024], replicated, may hold values from 0.25 to 1.75
- final_gain: bfloat16 [1024], replicated, may hold values from 0.25 to 1.75
- w_query: bfloat16 [1024, 1024], P(None, 'tp'), may hold values from -0.1875 to 0.1875
- w_key: bfloat16 [1024, 1024], P(None, 'tp'), may hold values from -0.1875 to 0.1875
- w_value: bfloat16 [1024, 1024], P(None, 'tp'), may hold values from -0.1875 to 0.1875
- w_out: bfloat16 [1024, 1024], P('tp'), may hold values from -0.1875 to 0.1875
- w_gate: bfloat16 [1024, 2816], P(None, 'tp'), may hold values from -0.1875 to 0.1875
- w_up: bfloat16 [1024, 2816], P(None, 'tp'), may hold values from -0.1875 to 0.1875
- w_down: bfloat16 [2816, 1024], P('tp'), may hold values from -0.109375 to 0.109375
- lm_head: bfloat16 [1024, 32128], P(None, ('ctx', 'tp')), may hold values from -0.1875 to 0.1875
Outputs:
- prompt_out: bfloat16 [2048, 1024], P('ctx')
- logits: float32 [4, 32128], P(None, ('ctx', 'tp'))
- relaid_keys: bfloat16 [2048, 1024], P(('ctx', 'tp'))
- relaid_values: bfloat16 [2048, 1024], P(('ctx', 'tp'))
Inputs may be any that keep to these rules, and one draw needn't show every extreme that they name: `cache_request`: only the even requests have cached rows, which may lie on any devices. `segment_ids`: the tokens of a request are consecutive; a request holds at most 1024 of them, and one request holds exactly that many.
All inputs are finite; a program needn't handle non-finite values.
Results may differ from a plain program's by a relative error of at most 0.03.
Values may be sent and summed in bfloat16 or wider, within the bound.
A program may use at most 64 MiB of HBM per device.

v0:
```python
import jax
import jax.numpy as jnp
from jax import lax
from jax.sharding import PartitionSpec as P

DH = 64
epsilon = 1e-06
scale_factor = 0.125
negative = -1e30


def joined(part, axis, combine):
    gathered = jax.tree.map(lambda a: lax.all_gather(a, axis), part)

    def take(source):
        return jax.tree.map(lambda a: lax.dynamic_index_in_dim(a, source, 0, False), gathered)

    return lax.fori_loop(
        1, lax.axis_size(axis), lambda source, state: combine(state, take(source)), take(0)
    )


def rms_norm(states, gain):
    states = states.astype(jnp.float32)
    mean_square = jnp.mean(states * states, axis=-1, keepdims=True)
    return (states * lax.rsqrt(mean_square + epsilon) * gain.astype(jnp.float32)).astype(
        jnp.bfloat16
    )


def partial_attend(queries, keys, values, allowed):
    scores = (
        jnp.einsum("qhd,khd->qhk", queries, keys, preferred_element_type=jnp.float32) * scale_factor
    )
    scores = jnp.where(allowed[:, None, :], scores, negative)
    highest = jnp.max(scores, axis=2)
    weights = jnp.where(allowed[:, None, :], jnp.exp(scores - highest[:, :, None]), 0.0)
    weight_sum = jnp.sum(weights, axis=2)
    summed = jnp.einsum(
        "qhk,khd->qhd", weights.astype(jnp.bfloat16), values, preferred_element_type=jnp.float32
    )
    return (highest, weight_sum, summed)


def join_parts(earlier, latter):
    highest = jnp.maximum(earlier[0], latter[0])
    left_scale = jnp.exp(earlier[0] - highest)
    right_scale = jnp.exp(latter[0] - highest)
    weight_sum = earlier[1] * left_scale + latter[1] * right_scale
    summed = earlier[2] * left_scale[:, :, None] + latter[2] * right_scale[:, :, None]
    return (highest, weight_sum, summed)


def finish(partials):
    return (partials[2] / partials[1][:, :, None]).astype(jnp.bfloat16)


def fold_block(running, query_heads, block_keys, block_values, allowed):
    key_count = block_keys.shape[0]
    head_group = query_heads.shape[1]

    def attend(current):
        return join_parts(
            current,
            partial_attend(
                query_heads,
                block_keys.reshape(key_count, head_group, DH),
                block_values.reshape(key_count, head_group, DH),
                allowed,
            ),
        )

    def unchanged(current):
        return current

    return lax.cond(jnp.any(allowed), attend, unchanged, running)


def gated_units(normed, w_gate, w_up, w_down):
    gate_value = jnp.dot(normed, w_gate, preferred_element_type=jnp.float32)
    up_value = jnp.dot(normed, w_up, preferred_element_type=jnp.float32)
    hidden = (jax.nn.gelu(gate_value, approximate=True) * up_value).astype(jnp.bfloat16)
    return jnp.dot(hidden, w_down, preferred_element_type=jnp.float32)


def project(normed, weight):
    return jnp.dot(normed, weight, preferred_element_type=jnp.float32).astype(jnp.bfloat16)


def on_device(
    prompt_states,
    segment_ids,
    past_keys,
    past_values,
    cache_request,
    decode_ids,
    embed_table,
    attn_gain,
    ff_gain,
    final_gain,
    w_query,
    w_key,
    w_value,
    w_out,
    w_gate,
    w_up,
    w_down,
    lm_head,
):
    row_count = prompt_states.shape[0]
    head_group = w_query.shape[1] // DH
    ctx_index = lax.axis_index("ctx")
    normed = rms_norm(prompt_states, attn_gain)
    queries = project(normed, w_query)
    keys = project(normed, w_key)
    values = project(normed, w_value)
    query_heads = queries.reshape(row_count, head_group, DH)
    q_positions = ctx_index * row_count + jnp.arange(row_count, dtype=jnp.int32)
    start_parts = (
        jnp.full((row_count, head_group), negative, jnp.float32),
        jnp.zeros((row_count, head_group), jnp.float32),
        jnp.zeros((row_count, head_group, DH), jnp.float32),
    )
    block_keys = lax.all_gather(keys, "ctx", axis=0, tiled=True)
    block_values = lax.all_gather(values, "ctx", axis=0, tiled=True)
    block_segment = lax.all_gather(segment_ids, "ctx", axis=0, tiled=True)
    key_positions = jnp.arange(block_segment.shape[0], dtype=jnp.int32)
    partials = fold_block(
        start_parts,
        query_heads,
        block_keys,
        block_values,
        (segment_ids[:, None] == block_segment[None, :])
        & (key_positions[None, :] <= q_positions[:, None]),
    )
    block_keys = lax.all_gather(past_keys, "ctx", axis=0, tiled=True)
    block_values = lax.all_gather(past_values, "ctx", axis=0, tiled=True)
    block_segment = lax.all_gather(cache_request, "ctx", axis=0, tiled=True)
    partials = fold_block(
        partials,
        query_heads,
        block_keys,
        block_values,
        segment_ids[:, None] == block_segment[None, :],
    )
    attended = finish(partials).reshape(row_count, head_group * DH)
    head_term = jnp.dot(attended, w_out, preferred_element_type=jnp.float32)
    residual = prompt_states.astype(jnp.float32) + lax.psum(
        head_term.astype(jnp.bfloat16), "tp"
    ).astype(jnp.float32)
    unit_term = gated_units(rms_norm(residual, ff_gain), w_gate, w_up, w_down)
    prompt_out = (
        residual + lax.psum(unit_term.astype(jnp.bfloat16), "tp").astype(jnp.float32)
    ).astype(jnp.bfloat16)
    relaid_keys, relaid_values = (
        lax.all_to_all(keys, "tp", split_axis=0, concat_axis=1, tiled=True),
        lax.all_to_all(values, "tp", split_axis=0, concat_axis=1, tiled=True),
    )
    vocab_rows = embed_table.shape[0]
    vocab_start = lax.axis_index(("ctx", "tp")) * vocab_rows
    one_hot = (
        decode_ids[:, None] == vocab_start + jnp.arange(vocab_rows, dtype=jnp.int32)[None, :]
    ).astype(jnp.bfloat16)
    embedded = lax.psum(
        jnp.dot(one_hot, embed_table, preferred_element_type=jnp.float32), ("ctx", "tp")
    )
    request_count = decode_ids.shape[0]
    decode_normed = rms_norm(embedded, attn_gain)
    decode_queries = project(decode_normed, w_query)
    decode_heads = decode_queries.reshape(request_count, head_group, DH)
    decode_keys = project(decode_normed, w_key).reshape(request_count, head_group, DH)
    decode_values = project(decode_normed, w_value).reshape(request_count, head_group, DH)
    requests = jnp.arange(request_count, dtype=jnp.int32)
    cache_count = past_keys.shape[0]
    cache_part = partial_attend(
        decode_heads,
        past_keys.reshape(cache_count, head_group, DH),
        past_values.reshape(cache_count, head_group, DH),
        requests[:, None] == cache_request[None, :],
    )
    prompt_part = partial_attend(
        decode_heads,
        keys.reshape(row_count, head_group, DH),
        values.reshape(row_count, head_group, DH),
        requests[:, None] == segment_ids[None, :],
    )
    gathered = joined(join_parts(prompt_part, cache_part), "ctx", join_parts)
    own_part = partial_attend(
        decode_heads, decode_keys, decode_values, requests[:, None] == requests[None, :]
    )
    decode_attended = finish(join_parts(gathered, own_part)).reshape(request_count, head_group * DH)
    decode_residual = embedded + lax.psum(
        jnp.dot(decode_attended, w_out, preferred_element_type=jnp.float32), "tp"
    )
    decode_term = gated_units(rms_norm(decode_residual, ff_gain), w_gate, w_up, w_down)
    decode_final = decode_residual + lax.psum(decode_term, "tp")
    logits = jnp.dot(
        rms_norm(decode_final, final_gain), lm_head, preferred_element_type=jnp.float32
    )
    return (prompt_out, logits, relaid_keys, relaid_values)


def solution(mesh):
    placed = (
        P("ctx", None),
        P("ctx"),
        P("ctx", "tp"),
        P("ctx", "tp"),
        P("ctx"),
        P(),
        P(("ctx", "tp"), None),
        P(),
        P(),
        P(),
        P(None, "tp"),
        P(None, "tp"),
        P(None, "tp"),
        P("tp", None),
        P(None, "tp"),
        P(None, "tp"),
        P("tp", None),
        P(None, ("ctx", "tp")),
    )
    return jax.shard_map(
        on_device,
        mesh=mesh,
        in_specs=placed,
        out_specs=(
            P("ctx", None),
            P(None, ("ctx", "tp")),
            P(("ctx", "tp"), None),
            P(("ctx", "tp"), None),
        ),
        check_vma=False,
    )
```

profile of v0, /device:TPU:0, one launch (start us, length us, event | category | flops | bytes accessed | tf_op | source)
XLA Modules:
  0.0 462.5 jit_solution(8723615287294162902)
XLA Ops:
  7.3 25.5 %all-gather.2 = s32[16,1,128]{2,1,0:T(1,128)S(1)} all-gather(s32[1,1,128]{2,1,0:T(1,128)} %bitcast.173), channel_id=1, replica_groups=mesh['ctx'=16,'tp'=8] {'ctx'}, dimensions={0}, use_global_device_ids=true | all-gather | bytes 8704 | tf_op jit(solution)/shard_map/all_gather | solution.py:126
  32.8 19.3 %all-gather.1 = s32[16,1,128]{2,1,0:T(1,128)S(1)} all-gather(s32[1,1,128]{2,1,0:T(1,128)} %bitcast.174), channel_id=1, replica_groups=mesh['ctx'=16,'tp'=8] {'ctx'}, dimensions={0}, use_global_device_ids=true | all-gather | bytes 8704 | tf_op jit(solution)/shard_map/all_gather | solution.py:138
  52.1 3.4 fusion.125
  56.8 0.7 convert_element_type.100
  57.4 1.1 fusion.44
  58.5 1.9 convolution_convert_fusion.4
  60.5 23.8 %all_gather.34 = bf16[2048,128]{1,0:T(8,128)(2,1)S(1)} all-gather(bf16[128,128]{1,0:T(8,128)(2,1)} %convolution_convert_fusion.4), channel_id=1, replica_groups=mesh['ctx'=16,'tp'=8] {'ctx'}, dimensions={0}, use_global_device_ids=true | all-gather | bytes 557056 | tf_op jit(solution)/shard_map/all_gather | solution.py:124
  84.6 0.9 convolution_convert_fusion.2
  85.5 22.3 %all_gather.35 = bf16[2048,128]{1,0:T(8,128)(2,1)} all-gather(bf16[128,128]{1,0:T(8,128)(2,1)} %convolution_convert_fusion.2), channel_id=1, replica_groups=mesh['ctx'=16,'tp'=8] {'ctx'}, dimensions={0}, use_global_device_ids=true | all-gather | bytes 557056 | tf_op jit(solution)/shard_map/all_gather | solution.py:125
  108.0 25.2 %all_gather.36 = bf16[2048,128]{0,1:T(8,128)(2,1)} all-gather(bf16[128,128]{0,1:T(8,128)(2,1)S(1)} %copy.75), channel_id=1, replica_groups=mesh['ctx'=16,'tp'=8] {'ctx'}, dimensions={0}, use_global_device_ids=true | all-gather | bytes 557056 | tf_op jit(solution)/shard_map/all_gather | solution.py:136
  133.3 22.1 %all_gather.37 = bf16[2048,128]{0,1:T(8,128)(2,1)} all-gather(bf16[128,128]{0,1:T(8,128)(2,1)S(1)} %copy.76), channel_id=1, replica_groups=mesh['ctx'=16,'tp'=8] {'ctx'}, dimensions={0}, use_global_device_ids=true | all-gather | bytes 557056 | tf_op jit(solution)/shard_map/all_gather | solution.py:137
  155.4 8.3 %conditional.2 = (f32[128,2]{0,1:T(2,128)}, f32[128,2]{0,1:T(2,128)S(1)}, f32[128,2,64]{0,2,1:T(8,128)S(1)}) conditional(s32[]{:T(128)} %convert_element_type.99, () %tuple.45, (pred[128,2048]{0,1:T(8,128)(4,1)}, bf16[2048,128]{1,0:T(8,128)(2,1)S(1)}, bf16[128,2,64]{0,2,1:T(8,128)(2,1)S(1)}, bf16[2048,128]{1,0:T(8,128)(2,1)}) %tuple.100), branch_computations={%region_3.4_spmd, %region_4.7_spmd} | conditional | flops 138970624 | bytes 11384884 | solution.py:76
  155.4 1.0 copy.73
  156.5 1.8 fusion.131
  158.2 0.6 exponential_multiply_fusion
  159.2 0.7 multiply_add_fusion
  159.9 2.1 copy.74
  162.0 1.7 fusion.5
  163.8 3.6 conditional.3
  163.8 1.8 fusion.132
  165.6 0.4 fusion.14
  166.0 0.7 multiply_add_fusion.1
  166.7 0.7 fusion.16
  167.4 1.0 convolution_convert_fusion.1
  168.4 4.9 %all-to-all-start = ((bf16[8,16,128]{2,1,0:T(8,128)(2,1)}), bf16[8,16,128]{2,1,0:T(8,128)(2,1)S(1)}, u32[]{:S(2)}, u32[]{:S(2)}) async-start(bf16[8,16,128]{2,1,0:T(8,128)(2,1)} %bitcast.34), calls=%async_computation | async-start | bytes 65536 | tf_op jit(solution)/shard_map/all_to_all | solution.py:156
  173.4 0.9 copy.77
  174.3 0.9 copy.81
  175.4 66.9 %psum.37 = f32[4,1024]{1,0:T(4,128)S(1)} all-reduce(f32[4,1024]{1,0:T(4,128)S(1)} %fusion.70), channel_id=1, replica_groups=mesh['ctx'=16,'tp'=8] {'ctx','tp'}, use_global_device_ids=true, to_apply=%region_14.15 | all-reduce | flops 4096 | bytes 32768 | tf_op jit(solution)/shard_map/psum | solution.py:164
  242.5 1.1 convolution_convert_fusion.7
  243.6 1.1 convolution_convert_fusion.6
  244.8 1.2 convolution_convert_fusion.5
  246.8 22.7 %all_gather.38 = f32[16,4,2]{1,2,0:T(2,128)S(1)} all-gather(f32[1,4,2]{1,2,0:T(2,128)S(1)} %get-tuple-element.301), channel_id=1, replica_groups=mesh['ctx'=16,'tp'=8] {'ctx'}, dimensions={0}, use_global_device_ids=true | all-gather | bytes 544 | tf_op jit(solution)/shard_map/all_gather | solution.py:13
  269.5 19.2 %all_gather.39 = f32[16,4,2]{1,2,0:T(2,128)S(1)} all-gather(f32[1,4,2]{1,2,0:T(2,128)S(1)} %get-tuple-element.300), channel_id=1, replica_groups=mesh['ctx'=16,'tp'=8] {'ctx'}, dimensions={0}, use_global_device_ids=true | all-gather | bytes 544 | tf_op jit(solution)/shard_map/all_gather | solution.py:13
  289.1 22.3 %all-gather = f32[64,2,64]{2,1,0:T(2,128)S(1)} all-gather(f32[4,2,64]{2,1,0:T(2,128)S(1)} %copy.83), channel_id=2, replica_groups=mesh['ctx'=16,'tp'=8] {'ctx'}, dimensions={0}, use_global_device_ids=true | all-gather | bytes 34816 | tf_op jit(solution)/shard_map/all_gather | solution.py:13
  311.4 4.4 while.19
  316.6 31.3 %psum.38 = f32[4,1024]{1,0:T(4,128)S(1)} all-reduce(f32[4,1024]{1,0:T(4,128)S(1)} %fusion.136), channel_id=1, replica_groups=mesh['ctx'=16,'tp'=8] {'tp'}, use_global_device_ids=true, to_apply=%region_24.25 | all-reduce | flops 4096 | bytes 32768 | tf_op jit(solution)/shard_map/psum | solution.py:192
  348.4 0.7 fusion.42
  349.0 30.6 %psum.39 = f32[4,1024]{1,0:T(4,128)S(1)} all-reduce(f32[4,1024]{1,0:T(4,128)S(1)} %fusion.42), channel_id=1, replica_groups=mesh['ctx'=16,'tp'=8] {'tp'}, use_global_device_ids=true, to_apply=%region_26.27 | all-reduce | flops 4096 | bytes 32768 | tf_op jit(solution)/shard_map/psum | solution.py:196
  379.8 0.8 fusion.59
  380.6 1.2 multiply_reduce_fusion
  381.8 1.4 fusion.120
  383.2 1.7 convolution_convert_fusion
  384.9 3.3 all-to-all-start.1
  388.3 0.6 copy_bitcast_fusion.1
  388.9 5.6 %all-to-all-done.1 = bf16[8,16,128]{2,1,0:T(8,128)(2,1)S(1)} async-done(((bf16[8,16,128]{2,1,0:T(8,128)(2,1)}), bf16[8,16,128]{2,1,0:T(8,128)(2,1)S(1)}, u32[]{:S(2)}, u32[]{:S(2)}) %all-to-all-start.1) | async-done | bytes 32800 | tf_op jit(solution)/shard_map/all_to_all | solution.py:157
  394.5 0.6 copy_bitcast_fusion
  395.1 58.8 %all-reduce.5.cloned.1.call-done = bf16[128,1024]{1,0:T(8,128)(2,1)} async-done(((bf16[128,1024]{1,0:T(8,128)(2,1)}), bf16[128,1024]{1,0:T(8,128)(2,1)}) %all-reduce.5.cloned.1.call-update) | async-done | bytes 262160 | tf_op jit(solution)/shard_map/psum | solution.py:153
  453.9 1.8 add_convert_fusion
  (149 shorter events, 8.6 us)
Async XLA Ops:
  7.2 341.2 %copy-start = (bf16[352,1024]{1,0:T(8,128)(2,1)S(1)}, bf16[352,1024]{1,0:T(8,128)(2,1)}, u32[]{:S(2)}) copy-start(bf16[352,1024]{1,0:T(8,128)(2,1)} %param.40) | copy-start | bytes 2162692
  7.2 77.1 %copy-start.1 = (bf16[128,1024]{1,0:T(8,128)(2,1)S(1)}, bf16[128,1024]{1,0:T(8,128)(2,1)}, u32[]{:S(2)}) copy-start(bf16[128,1024]{1,0:T(8,128)(2,1)} %param.24) | copy-start | bytes 786436
  7.2 77.1 %copy-start.10 = (bf16[1024,128]{1,0:T(8,128)(2,1)S(1)}, bf16[1024,128]{1,0:T(8,128)(2,1)}, u32[]{:S(2)}) copy-start(bf16[1024,128]{1,0:T(8,128)(2,1)} %param.34) | copy-start | bytes 786436
  7.2 77.4 %copy-start.11 = (bf16[1024,128]{1,0:T(8,128)(2,1)S(1)}, bf16[1024,128]{1,0:T(8,128)(2,1)}, u32[]{:S(2)}) copy-start(bf16[1024,128]{1,0:T(8,128)(2,1)} %param.36) | copy-start | bytes 786436
  7.2 100.6 %copy-start.12 = (bf16[128,128]{1,0:T(8,128)(2,1)S(1)}, bf16[128,128]{1,0:T(8,128)(2,1)}, u32[]{:S(2)}) copy-start(bf16[128,128]{1,0:T(8,128)(2,1)} %param.26) | copy-start | bytes 98308
  7.2 373.4 %all-reduce.3.cloned.1.call-start = ((), (), s32[]{:S(2)}) async-start(), calls=%async_computation.2 | async-start | bytes 524288 | tf_op jit(solution)/shard_map/psum | solution.py:148
  55.5 77.7 %copy-start.13 = (bf16[128,128]{1,0:T(8,128)(2,1)S(1)}, bf16[128,128]{1,0:T(8,128)(2,1)}, u32[]{:S(2)}) copy-start(bf16[128,128]{1,0:T(8,128)(2,1)} %param.27) | copy-start | bytes 98308
  156.4 2.4 copy-start.5
  163.7 3.7 copy-start.6
  163.7 9.7 %copy-start.18 = (s32[128]{0:T(128)S(1)}, s32[128]{0:T(128)}, u32[]{:S(2)}) copy-start(s32[128]{0:T(128)} %param.28) | copy-start | bytes 1540
  163.7 10.5 %copy-start.16 = (s32[128]{0:T(128)S(1)}, s32[128]{0:T(128)}, u32[]{:S(2)}) copy-start(s32[128]{0:T(128)} %param.25) | copy-start | bytes 1540
  163.7 11.4 %copy-start.7 = (bf16[251,1024]{1,0:T(8,128)(2,1)S(1)}, bf16[251,1024]{1,0:T(8,128)(2,1)}, u32[]{:S(2)}) copy-start(bf16[251,1024]{1,0:T(8,128)(2,1)} %param.30) | copy-start | bytes 1542148
  163.7 11.4 %copy-start.17 = (s32[4]{0:T(128)S(1)}, s32[4]{0:T(128)}, u32[]{:S(2)}) copy-start(s32[4]{0:T(128)} %param.29) | copy-start | bytes 52
  163.8 2.9 copy-start.9
  167.4 78.5 %copy-start.14 = (bf16[1024]{0:T(1024)(128)(2,1)S(1)}, bf16[1024]{0:T(1024)(128)(2,1)}, u32[]{:S(2)}) copy-start(bf16[1024]{0:T(1024)(128)(2,1)} %param.32) | copy-start | bytes 6148
  167.4 180.7 %copy-start.3 = (bf16[1024,352]{0,1:T(8,128)(2,1)S(1)}, bf16[1024,352]{0,1:T(8,128)(2,1)}, u32[]{:S(2)}) copy-start(bf16[1024,352]{0,1:T(8,128)(2,1)} %param.38) | copy-start | bytes 2162692
  168.4 180.0 %copy-start.4 = (bf16[1024,352]{0,1:T(8,128)(2,1)S(1)}, bf16[1024,352]{0,1:T(8,128)(2,1)}, u32[]{:S(2)}) copy-start(bf16[1024,352]{0,1:T(8,128)(2,1)} %param.39) | copy-start | bytes 2162692
  168.4 216.5 %all-to-all-start = ((bf16[8,16,128]{2,1,0:T(8,128)(2,1)}), bf16[8,16,128]{2,1,0:T(8,128)(2,1)S(1)}, u32[]{:S(2)}, u32[]{:S(2)}) async-start(bf16[8,16,128]{2,1,0:T(8,128)(2,1)} %bitcast.34), calls=%async_computation | async-start | bytes 65536 | tf_op jit(solution)/shard_map/all_to_all | solution.py:156
  173.3 280.5 %all-reduce.5.cloned.1.call-start = ((), (), s32[]{:S(2)}) async-start(), calls=%async_computation.3 | async-start | bytes 524288 | tf_op jit(solution)/shard_map/psum | solution.py:153
  244.7 135.1 %copy-start.15 = (bf16[1024]{0:T(1024)(128)(2,1)S(1)}, bf16[1024]{0:T(1024)(128)(2,1)}, u32[]{:S(2)}) copy-start(bf16[1024]{0:T(1024)(128)(2,1)} %param.33) | copy-start | bytes 6148
  244.7 135.1 %copy-start.8 = (bf16[1024,251]{1,0:T(8,128)(2,1)S(1)}, bf16[1024,251]{1,0:T(8,128)(2,1)}, u32[]{:S(2)}) copy-start(bf16[1024,251]{1,0:T(8,128)(2,1)} %param.41) | copy-start | bytes 1542148
  380.6 2.6 copy-start.2
  384.9 9.5 %all-to-all-start.1 = ((bf16[8,16,128]{2,1,0:T(8,128)(2,1)}), bf16[8,16,128]{2,1,0:T(8,128)(2,1)S(1)}, u32[]{:S(2)}, u32[]{:S(2)}) async-start(bf16[8,16,128]{2,1,0:T(8,128)(2,1)} %bitcast.36), calls=%async_computation.1 | async-start | bytes 65536 | tf_op jit(solution)/shard_map/all_to_all | solution.py:157
Sparse Core Ops, SparseCore 0:
  168.5 73.1 all-reduce.2
  385.0 68.7 all-reduce.4
where the time goes:
time: 464 us; the launch traced here: 462 us
  blocking collectives  331 us (71%)
  waiting for transfers between devices  64.4 us (14%)
  matrix products  19.7 us (4%)
  between operations  15.7 us (3%)
  other arithmetic  13.4 us (3%)
  local copies, waits for them, and re-layouts  9.55 us (2%)
  starting transfers between devices  8.32 us (2%)
    psum x1, blocking collectives, on_device(): lax.psum(jnp.dot(one_hot, embed_table, preferred_element_type=jnp.float32...  66.9 us
    all_gather x3, blocking collectives, joined(): gathered = jax.tree.map(lambda a: lax.all_gather(a, axis), part)  64.2 us
    psum x1, waiting for transfers between devices, on_device(): lax.psum(unit_term.astype(jnp.bfloat16), 'tp').astype(jnp.float32)  58.8 us
    psum x1, blocking collectives, on_device(): lax.psum(jnp.dot(decode_attended, w_out, preferred_element_type=jnp.float...  31.3 us
    psum x1, blocking collectives, on_device(): decode_final = decode_residual + lax.psum(decode_term, 'tp')  30.6 us
    all_gather x1, blocking collectives, on_device(): block_segment = lax.all_gather(segment_ids, 'ctx', axis=0, tiled=True)  25.5 us
    all_gather x1, blocking collectives, on_device(): block_keys = lax.all_gather(past_keys, 'ctx', axis=0, tiled=True)  25.2 us
    all_gather x1, blocking collectives, on_device(): block_keys = lax.all_gather(keys, 'ctx', axis=0, tiled=True)  23.8 us
  transfers between devices with their start and end apart: 4, of which 2 were waited for; matrix products, arithmetic and copies ran while one was open for 4% of the time, Pallas kernels for 0%

commit v1 on v0

--- a/solution.py
+++ b/solution.py
@@ -189,8 +189,9 @@
         decode_heads, decode_keys, decode_values, requests[:, None] == requests[None, :]
     )
     decode_attended = finish(join_parts(gathered, own_part)).reshape(request_count, head_group * DH)
-    decode_residual = embedded + lax.psum(
-        jnp.dot(decode_attended, w_out, preferred_element_type=jnp.float32), "tp"
+    decode_residual = embedded + jnp.sum(
+        lax.all_gather(jnp.dot(decode_attended, w_out, preferred_element_type=jnp.float32), "tp"),
+        axis=0,
     )
     decode_term = gated_units(rms_norm(decode_residual, ff_gain), w_gate, w_up, w_down)
     decode_final = decode_residual + lax.psum(decode_term, "tp")

time: 464 us -> 461 us (level)
    psum x1 -> x0, blocking collectives: 31.3 us -> none  [on_device(): lax.psum(jnp.dot(decode_attended, w_out, preferred_element_type=jnp.float...]
    all_gather x0 -> x1, blocking collectives: none -> 28.2 us  [on_device(): lax.all_gather(jnp.dot(decode_attended, w_out, preferred_element_type=jnp...]
where the time goes in v1:
time: 461 us; the launch traced here: 460 us
  blocking collectives  329 us (71%)
  waiting for transfers between devices  64.6 us (14%)
  matrix products  19.6 us (4%)
  between operations  15.7 us (3%)
  other arithmetic  13.4 us (3%)
  local copies, waits for them, and re-layouts  9.62 us (2%)
  starting transfers between devices  8.19 us (2%)
    psum x1, blocking collectives, on_device(): lax.psum(jnp.dot(one_hot, embed_table, preferred_element_type=jnp.float32...  67 us
    all_gather x3, blocking collectives, joined(): gathered = jax.tree.map(lambda a: lax.all_gather(a, axis), part)  64.1 us
    psum x1, waiting for transfers between devices, on_device(): lax.psum(unit_term.astype(jnp.bfloat16), 'tp').astype(jnp.float32)  58.9 us
    psum x1, blocking collectives, on_device(): decode_final = decode_residual + lax.psum(decode_term, 'tp')  31.4 us
    all_gather x1, blocking collectives, on_device(): lax.all_gather(jnp.dot(decode_attended, w_out, preferred_element_type=jnp...  28.2 us
    all_gather x1, blocking collectives, on_device(): block_segment = lax.all_gather(segment_ids, 'ctx', axis=0, tiled=True)  25.5 us
    all_gather x1, blocking collectives, on_device(): block_keys = lax.all_gather(past_keys, 'ctx', axis=0, tiled=True)  25.2 us
    all_gather x1, blocking collectives, on_device(): block_keys = lax.all_gather(keys, 'ctx', axis=0, tiled=True)  23.8 us
  transfers between devices with their start and end apart: 4, of which 2 were waited for; matrix products, arithmetic and copies ran while one was open for 4% of the time, Pallas kernels for 0%

profile of v1, /device:TPU:0, one launch (start us, length us, event | category | flops | bytes accessed | tf_op | source)
XLA Modules:
  0.0 460.1 jit_solution(3018082631574060940)
XLA Ops:
  7.3 25.5 %all-gather.3 = s32[16,1,128]{2,1,0:T(1,128)S(1)} all-gather(s32[1,1,128]{2,1,0:T(1,128)} %bitcast.175), channel_id=1, replica_groups=mesh['ctx'=16,'tp'=8] {'ctx'}, dimensions={0}, use_global_device_ids=true | all-gather | bytes 8704 | tf_op jit(solution)/shard_map/all_gather | solution.py:126
  32.8 19.3 %all-gather.2 = s32[16,1,128]{2,1,0:T(1,128)S(1)} all-gather(s32[1,1,128]{2,1,0:T(1,128)} %bitcast.176), channel_id=1, replica_groups=mesh['ctx'=16,'tp'=8] {'ctx'}, dimensions={0}, use_global_device_ids=true | all-gather | bytes 8704 | tf_op jit(solution)/shard_map/all_gather | solution.py:138
  52.1 3.4 fusion.125
  56.8 0.7 convert_element_type.100
  57.4 1.1 fusion.44
  58.5 1.9 convolution_convert_fusion.4
  60.5 23.8 %all_gather.40 = bf16[2048,128]{1,0:T(8,128)(2,1)S(1)} all-gather(bf16[128,128]{1,0:T(8,128)(2,1)} %convolution_convert_fusion.4), channel_id=1, replica_groups=mesh['ctx'=16,'tp'=8] {'ctx'}, dimensions={0}, use_global_device_ids=true | all-gather | bytes 557056 | tf_op jit(solution)/shard_map/all_gather | solution.py:124
  84.6 0.9 convolution_convert_fusion.2
  85.5 22.3 %all_gather.41 = bf16[2048,128]{1,0:T(8,128)(2,1)} all-gather(bf16[128,128]{1,0:T(8,128)(2,1)} %convolution_convert_fusion.2), channel_id=1, replica_groups=mesh['ctx'=16,'tp'=8] {'ctx'}, dimensions={0}, use_global_device_ids=true | all-gather | bytes 557056 | tf_op jit(solution)/shard_map/all_gather | solution.py:125
  108.0 25.2 %all_gather.42 = bf16[2048,128]{0,1:T(8,128)(2,1)} all-gather(bf16[128,128]{0,1:T(8,128)(2,1)S(1)} %copy.75), channel_id=1, replica_groups=mesh['ctx'=16,'tp'=8] {'ctx'}, dimensions={0}, use_global_device_ids=true | all-gather | bytes 557056 | tf_op jit(solution)/shard_map/all_gather | solution.py:136
  133.3 22.1 %all_gather.43 = bf16[2048,128]{0,1:T(8,128)(2,1)} all-gather(bf16[128,128]{0,1:T(8,128)(2,1)S(1)} %copy.76), channel_id=1, replica_groups=mesh['ctx'=16,'tp'=8] {'ctx'}, dimensions={0}, use_global_device_ids=true | all-gather | bytes 557056 | tf_op jit(solution)/shard_map/all_gather | solution.py:137
  155.4 8.3 %conditional.2 = (f32[128,2]{0,1:T(2,128)}, f32[128,2]{0,1:T(2,128)S(1)}, f32[128,2,64]{0,2,1:T(8,128)S(1)}) conditional(s32[]{:T(128)} %convert_element_type.99, () %tuple.45, (pred[128,2048]{0,1:T(8,128)(4,1)}, bf16[2048,128]{1,0:T(8,128)(2,1)S(1)}, bf16[128,2,64]{0,2,1:T(8,128)(2,1)S(1)}, bf16[2048,128]{1,0:T(8,128)(2,1)}) %tuple.100), branch_computations={%region_3.4_spmd, %region_4.7_spmd} | conditional | flops 138970624 | bytes 11384884 | solution.py:76
  155.4 1.0 copy.73
  156.5 1.8 fusion.131
  158.2 0.6 exponential_multiply_fusion
  159.2 0.7 multiply_add_fusion
  159.9 2.1 copy.74
  162.0 1.7 fusion.5
  163.8 3.6 conditional.3
  163.8 1.8 fusion.132
  165.6 0.4 fusion.14
  166.0 0.7 multiply_add_fusion.1
  166.7 0.7 fusion.16
  167.4 1.0 convolution_convert_fusion.1
  168.4 4.8 %all-to-all-start = ((bf16[8,16,128]{2,1,0:T(8,128)(2,1)}), bf16[8,16,128]{2,1,0:T(8,128)(2,1)S(1)}, u32[]{:S(2)}, u32[]{:S(2)}) async-start(bf16[8,16,128]{2,1,0:T(8,128)(2,1)} %bitcast.35), calls=%async_computation | async-start | bytes 65536 | tf_op jit(solution)/shard_map/all_to_all | solution.py:156
  173.3 0.9 copy.77
  174.2 0.9 copy.81
  175.3 67.0 %psum.30 = f32[4,1024]{1,0:T(4,128)S(1)} all-reduce(f32[4,1024]{1,0:T(4,128)S(1)} %fusion.70), channel_id=1, replica_groups=mesh['ctx'=16,'tp'=8] {'ctx','tp'}, use_global_device_ids=true, to_apply=%region_14.15 | all-reduce | flops 4096 | bytes 32768 | tf_op jit(solution)/shard_map/psum | solution.py:164
  242.5 1.1 convolution_convert_fusion.7
  243.6 1.1 convolution_convert_fusion.6
  244.7 1.1 convolution_convert_fusion.5
  246.7 22.5 %all_gather.44 = f32[16,4,2]{1,2,0:T(2,128)S(1)} all-gather(f32[1,4,2]{1,2,0:T(2,128)S(1)} %get-tuple-element.301), channel_id=1, replica_groups=mesh['ctx'=16,'tp'=8] {'ctx'}, dimensions={0}, use_global_device_ids=true | all-gather | bytes 544 | tf_op jit(solution)/shard_map/all_gather | solution.py:13
  269.3 19.2 %all_gather.45 = f32[16,4,2]{1,2,0:T(2,128)S(1)} all-gather(f32[1,4,2]{1,2,0:T(2,128)S(1)} %get-tuple-element.300), channel_id=1, replica_groups=mesh['ctx'=16,'tp'=8] {'ctx'}, dimensions={0}, use_global_device_ids=true | all-gather | bytes 544 | tf_op jit(solution)/shard_map/all_gather | solution.py:13
  288.9 22.3 %all-gather = f32[64,2,64]{2,1,0:T(2,128)S(1)} all-gather(f32[4,2,64]{2,1,0:T(2,128)S(1)} %copy.83), channel_id=2, replica_groups=mesh['ctx'=16,'tp'=8] {'ctx'}, dimensions={0}, use_global_device_ids=true | all-gather | bytes 34816 | tf_op jit(solution)/shard_map/all_gather | solution.py:13
  311.2 4.4 while.19
  316.4 28.2 %all-gather.4 = f32[8,4,1024]{2,1,0:T(4,128)S(1)} all-gather(f32[1,4,1024]{2,1,0:T(4,128)S(1)} %convolution_bitcast_fusion.2), channel_id=3, replica_groups=mesh['ctx'=16,'tp'=8] {'tp'}, dimensions={0}, use_global_device_ids=true | all-gather | bytes 147456 | tf_op jit(solution)/shard_map/all_gather | solution.py:193
  345.0 0.7 fusion.42
  345.7 31.4 %psum.31 = f32[4,1024]{1,0:T(4,128)S(1)} all-reduce(f32[4,1024]{1,0:T(4,128)S(1)} %fusion.42), channel_id=1, replica_groups=mesh['ctx'=16,'tp'=8] {'tp'}, use_global_device_ids=true, to_apply=%region_26.27 | all-reduce | flops 4096 | bytes 32768 | tf_op jit(solution)/shard_map/psum | solution.py:197
  377.2 0.8 fusion.59
  378.1 1.2 multiply_reduce_fusion
  379.3 1.4 fusion.120
  380.6 1.7 convolution_convert_fusion
  382.3 3.3 all-to-all-start.1
  385.7 0.6 copy_bitcast_fusion.1
  386.3 5.6 %all-to-all-done.1 = bf16[8,16,128]{2,1,0:T(8,128)(2,1)S(1)} async-done(((bf16[8,16,128]{2,1,0:T(8,128)(2,1)}), bf16[8,16,128]{2,1,0:T(8,128)(2,1)S(1)}, u32[]{:S(2)}, u32[]{:S(2)}) %all-to-all-start.1) | async-done | bytes 32800 | tf_op jit(solution)/shard_map/all_to_all | solution.py:157
  391.9 0.6 copy_bitcast_fusion
  392.5 58.9 %all-reduce.5.cloned.1.call-done = bf16[128,1024]{1,0:T(8,128)(2,1)} async-done(((bf16[128,1024]{1,0:T(8,128)(2,1)}), bf16[128,1024]{1,0:T(8,128)(2,1)}) %all-reduce.5.cloned.1.call-update) | async-done | bytes 262160 | tf_op jit(solution)/shard_map/psum | solution.py:153
  451.4 1.8 add_convert_fusion
  (150 shorter events, 8.6 us)
Async XLA Ops:
  7.2 337.9 %copy-start = (bf16[352,1024]{1,0:T(8,128)(2,1)S(1)}, bf16[352,1024]{1,0:T(8,128)(2,1)}, u32[]{:S(2)}) copy-start(bf16[352,1024]{1,0:T(8,128)(2,1)} %param.40) | copy-start | bytes 2162692
  7.2 77.1 %copy-start.1 = (bf16[128,1024]{1,0:T(8,128)(2,1)S(1)}, bf16[128,1024]{1,0:T(8,128)(2,1)}, u32[]{:S(2)}) copy-start(bf16[128,1024]{1,0:T(8,128)(2,1)} %param.24) | copy-start | bytes 786436
  7.2 77.1 %copy-start.10 = (bf16[1024,128]{1,0:T(8,128)(2,1)S(1)}, bf16[1024,128]{1,0:T(8,128)(2,1)}, u32[]{:S(2)}) copy-start(bf16[1024,128]{1,0:T(8,128)(2,1)} %param.34) | copy-start | bytes 786436
  7.2 77.4 %copy-start.11 = (bf16[1024,128]{1,0:T(8,128)(2,1)S(1)}, bf16[1024,128]{1,0:T(8,128)(2,1)}, u32[]{:S(2)}) copy-start(bf16[1024,128]{1,0:T(8,128)(2,1)} %param.36) | copy-start | bytes 786436
  7.2 100.6 %copy-start.12 = (bf16[128,128]{1,0:T(8,128)(2,1)S(1)}, bf16[128,128]{1,0:T(8,128)(2,1)}, u32[]{:S(2)}) copy-start(bf16[128,128]{1,0:T(8,128)(2,1)} %param.26) | copy-start | bytes 98308
  7.2 370.8 %all-reduce.3.cloned.1.call-start = ((), (), s32[]{:S(2)}) async-start(), calls=%async_computation.2 | async-start | bytes 524288 | tf_op jit(solution)/shard_map/psum | solution.py:148
  55.5 77.7 %copy-start.13 = (bf16[128,128]{1,0:T(8,128)(2,1)S(1)}, bf16[128,128]{1,0:T(8,128)(2,1)}, u32[]{:S(2)}) copy-start(bf16[128,128]{1,0:T(8,128)(2,1)} %param.27) | copy-start | bytes 98308
  156.4 2.4 copy-start.5
  163.7 3.7 copy-start.6
  163.7 9.5 %copy-start.18 = (s32[128]{0:T(128)S(1)}, s32[128]{0:T(128)}, u32[]{:S(2)}) copy-start(s32[128]{0:T(128)} %param.28) | copy-start | bytes 1540
  163.7 10.5 %copy-start.16 = (s32[128]{0:T(128)S(1)}, s32[128]{0:T(128)}, u32[]{:S(2)}) copy-start(s32[128]{0:T(128)} %param.25) | copy-start | bytes 1540
  163.7 11.4 %copy-start.7 = (bf16[251,1024]{1,0:T(8,128)(2,1)S(1)}, bf16[251,1024]{1,0:T(8,128)(2,1)}, u32[]{:S(2)}) copy-start(bf16[251,1024]{1,0:T(8,128)(2,1)} %param.30) | copy-start | bytes 1542148
  163.7 11.4 %copy-start.17 = (s32[4]{0:T(128)S(1)}, s32[4]{0:T(128)}, u32[]{:S(2)}) copy-start(s32[4]{0:T(128)} %param.29) | copy-start | bytes 52
  163.8 2.9 copy-start.9
  167.4 78.5 %copy-start.14 = (bf16[1024]{0:T(1024)(128)(2,1)S(1)}, bf16[1024]{0:T(1024)(128)(2,1)}, u32[]{:S(2)}) copy-start(bf16[1024]{0:T(1024)(128)(2,1)} %param.32) | copy-start | bytes 6148
  167.4 177.3 %copy-start.3 = (bf16[1024,352]{0,1:T(8,128)(2,1)S(1)}, bf16[1024,352]{0,1:T(8,128)(2,1)}, u32[]{:S(2)}) copy-start(bf16[1024,352]{0,1:T(8,128)(2,1)} %param.38) | copy-start | bytes 2162692
  168.4 213.9 %all-to-all-start = ((bf16[8,16,128]{2,1,0:T(8,128)(2,1)}), bf16[8,16,128]{2,1,0:T(8,128)(2,1)S(1)}, u32[]{:S(2)}, u32[]{:S(2)}) async-start(bf16[8,16,128]{2,1,0:T(8,128)(2,1)} %bitcast.35), calls=%async_computation | async-start | bytes 65536 | tf_op jit(solution)/shard_map/all_to_all | solution.py:156
  173.2 278.3 %all-reduce.5.cloned.1.call-start = ((), (), s32[]{:S(2)}) async-start(), calls=%async_computation.3 | async-start | bytes 524288 | tf_op jit(solution)/shard_map/psum | solution.py:153
  173.3 171.8 %copy-start.4 = (bf16[1024,352]{0,1:T(8,128)(2,1)S(1)}, bf16[1024,352]{0,1:T(8,128)(2,1)}, u32[]{:S(2)}) copy-start(bf16[1024,352]{0,1:T(8,128)(2,1)} %param.39) | copy-start | bytes 2162692
  245.8 131.4 %copy-start.15 = (bf16[1024]{0:T(1024)(128)(2,1)S(1)}, bf16[1024]{0:T(1024)(128)(2,1)}, u32[]{:S(2)}) copy-start(bf16[1024]{0:T(1024)(128)(2,1)} %param.33) | copy-start | bytes 6148
  245.8 131.4 %copy-start.8 = (bf16[1024,251]{1,0:T(8,128)(2,1)S(1)}, bf16[1024,251]{1,0:T(8,128)(2,1)}, u32[]{:S(2)}) copy-start(bf16[1024,251]{1,0:T(8,128)(2,1)} %param.41) | copy-start | bytes 1542148
  378.1 2.6 copy-start.2
  382.3 9.5 %all-to-all-start.1 = ((bf16[8,16,128]{2,1,0:T(8,128)(2,1)}), bf16[8,16,128]{2,1,0:T(8,128)(2,1)S(1)}, u32[]{:S(2)}, u32[]{:S(2)}) async-start(bf16[8,16,128]{2,1,0:T(8,128)(2,1)} %bitcast.37), calls=%async_computation.1 | async-start | bytes 65536 | tf_op jit(solution)/shard_map/all_to_all | solution.py:157
Sparse Core Ops, SparseCore 0:
  168.5 73.0 all-reduce.2
  382.4 68.9 all-reduce.4
